TPU v7x, 32 devices: a whole 2x2x4 slice. The times are simulated.
32 devices in a mesh: groups: 2 (over y), seq: 4 (over z), mp: 2 (over x), rep: 2 (over core).
Axes of the slice: x: 2, y: 2, z: 4, core: 2. Of those that a mesh axis runs over, the one named last changes fastest.
Arguments:
- tokens: bfloat16 [8192, 2240], P(('groups', 'seq', 'rep')), parts along dimension 0, may hold values from -8 to 8
- slot_image: int32 [32], P(('groups', 'seq', 'rep')), parts along dimension 0, may hold values from 0 to 5, as said below
- modulation: float32 [12, 3, 2240], P('groups'), parts along dimension 0, may hold values from -3 to 3
- w_qkv: bfloat16 [2240, 3, 1280], P('rep', None, 'mp'), may hold values from -0.125 to 0.125
- w_out: bfloat16 [1280, 2240], P('rep', 'mp'), may hold values from -0.15625 to 0.15625
Outputs:
- updated: bfloat16 [8192, 2240], P(('groups', 'seq', 'rep'), 'mp'), parts along dimension 0
There are 2 independent parts, one for each index of `groups`. A program takes and returns all parts, laid end to end along the dimension named above; an argument that names none is the same for every part. Nothing has to cross between parts.
Inputs may be any that keep to these rules, and one draw needn't show every extreme that they name: `slot_image`: every one of the 6 images owns one tile slot or more.
All inputs are finite; a program needn't handle non-finite values.
Results may differ from a plain program's by a relative error of at most 0.0036.
Values may be sent and summed in bfloat16 or wider, within the bound.
No kernel may reach another device: no remote copies, remote signals or barrier semaphores. Data moves between devices by JAX's collectives and lax.ppermute only.
A program may use at most 128 MiB of HBM per device.

v0:
```python
import jax
import jax.numpy as jnp
from jax import lax
from jax.sharding import PartitionSpec as P

D = 2240
HD = 32


def body(tokens, slot_image, modulation, w_qkv, w_out):
    hi = lax.Precision.HIGHEST
    tiles = slot_image.shape[0]
    rows = tokens.shape[0]
    tile_len = rows // tiles
    images = modulation.shape[0]
    width = w_qkv.shape[2]
    per_dev = width // HD
    picker = (slot_image[:, None] == jnp.arange(images, dtype=jnp.int32)[None, :]).astype(
        jnp.float32
    )
    per_tile = jnp.dot(picker, modulation.reshape(images, 3 * D), precision=hi).reshape(tiles, 3, D)
    xf = tokens.astype(jnp.float32).reshape(tiles, tile_len, D)
    mean = jnp.mean(xf, axis=2, keepdims=True)
    var = jnp.mean((xf - mean) ** 2, axis=2, keepdims=True)
    normed = (xf - mean) / jnp.sqrt(var + 1e-06)
    modulated = (normed * (1.0 + per_tile[:, None, 1, :]) + per_tile[:, None, 0, :]).astype(
        jnp.bfloat16
    )
    modulated = modulated.reshape(rows, D)
    qkv = jnp.einsum(
        "td,dcm->tcm",
        modulated,
        lax.all_gather(w_qkv, "rep", axis=0, tiled=True),
        preferred_element_type=jnp.float32,
    )
    qkv = qkv.reshape(tiles, tile_len, 3, per_dev, HD)
    query = jax.nn.relu(qkv[:, :, 0]).astype(jnp.bfloat16)
    keyf = jax.nn.relu(qkv[:, :, 1]).astype(jnp.bfloat16)
    value = qkv[:, :, 2].astype(jnp.bfloat16)
    tile_state = jnp.einsum("slhe,slhf->shef", keyf, value, preferred_element_type=jnp.float32)
    tile_ksum = jnp.sum(keyf.astype(jnp.float32), axis=1)
    state = jnp.einsum("si,shef->ihef", picker, tile_state, precision=hi)
    ksum = jnp.einsum("si,she->ihe", picker, tile_ksum, precision=hi)
    state, ksum = lax.psum((state, ksum), ("seq", "rep"))
    own_state = jnp.einsum("si,ihef->shef", picker, state, precision=hi)
    own_ksum = jnp.einsum("si,ihe->she", picker, ksum, precision=hi)
    query_wide = query.astype(jnp.float32)
    numer = jnp.einsum("slhe,shef->slhf", query_wide, own_state, precision=hi)
    denom = jnp.einsum("slhe,she->slh", query_wide, own_ksum, precision=hi) + 1e-06
    attn = (numer / denom[..., None]).astype(jnp.bfloat16).reshape(rows, per_dev * HD)
    out_full = lax.all_gather(w_out, "rep", axis=0, tiled=True)
    cols = out_full.shape[1]
    projected = jnp.dot(
        lax.all_gather(attn, "mp", axis=1, tiled=True), out_full, preferred_element_type=jnp.float32
    )
    offset = lax.axis_index("mp") * cols
    own_tokens = (
        lax.dynamic_slice_in_dim(tokens, offset, cols, 1)
        .astype(jnp.float32)
        .reshape(tiles, tile_len, cols)
    )
    gate = lax.dynamic_slice_in_dim(per_tile[:, 2, :], offset, cols, 1)
    updated = own_tokens + gate[:, None, :] * projected.reshape(tiles, tile_len, cols)
    return updated.astype(jnp.bfloat16).reshape(rows, cols)


def solution(mesh):
    return jax.shard_map(
        body,
        mesh=mesh,
        in_specs=(
            P(("groups", "seq", "rep"), None),
            P(("groups", "seq", "rep")),
            P("groups", None, None),
            P("rep", None, "mp"),
            P("rep", "mp"),
        ),
        out_specs=P(("groups", "seq", "rep"), "mp"),
        check_vma=False,
    )
```

profile of v0, /device:TPU:0, one launch (start us, length us, event | category | flops | bytes accessed | tf_op | source)
XLA Modules:
  0.0 175.1 jit_solution(10275999285317942195)
XLA Ops:
  6.5 0.7 all-gather.4.cloned.1.call-update
  7.3 0.0 all-reduce.2.cloned.1.call-start
  7.3 0.2 copy-done.1
  7.5 0.2 reshape.54
  7.7 0.1 dot_general.41
  7.8 0.3 fusion.24
  8.1 0.4 copy.12
  8.5 2.7 %mul.34 = f32[2,256,2240]{1,0,2:T(2,128)S(1)} broadcast(f32[2,2240]{0,1:T(8,128)S(1)} %copy.12), dimensions={0,2} | broadcast | bytes 4605440 | tf_op jit(solution)/shard_map/mul | solution.py:26
  11.3 2.6 %copy.34 = f32[280,8,2,256]{3,1,2,0:T(8,128)} copy(f32[280,8,2,256]{3,2,1,0:T(2,128)S(1)} %bitcast.80) | data formatting | bytes 9175040
  13.8 0.4 copy.13
  14.2 0.0 slice-start
  14.2 2.7 %add.57 = f32[2,256,2240]{1,0,2:T(2,128)S(1)} broadcast(f32[2,2240]{0,1:T(8,128)S(1)} %copy.13), dimensions={0,2} | broadcast | bytes 4605440 | tf_op jit(solution)/shard_map/add | solution.py:26
  17.0 0.0 copy-start
  17.0 0.0 slice-start.1
  17.0 0.5 copy.35
  17.5 1.5 copy-done
  19.0 0.4 convert_reduce_fusion
  19.4 0.7 fusion.2
  20.1 3.0 %fusion.5 = bf16[512,2240]{0,1:T(8,128)(2,1)} fusion(f32[512,2240]{0,1:T(8,128)S(1)} %bitcast.79, f32[512,2240]{0,1:T(8,128)S(1)} %bitcast.78, bf16[512,2240]{0,1:T(8,128)(2,1)S(1)} %copy-done, f32[512]{0:T(512)S(1)} %add_sqrt_fusion, f32[512]{0:T(512)S(1)} %broadcast_multiply_fusion), kind=kLoop, calls=%fused_computation.7 | loop fusion | flops 6881280 | bytes 13766656 | tf_op jit(solution)/shard_map/convert_element_type | solution.py:26
  23.1 6.1 %dot_general.43 = bf16[2,256,2240]{1,0,2:T(2,128)(2,1)} reshape(bf16[512,2240]{0,1:T(8,128)(2,1)} %fusion.5) | data formatting | bytes 4587520 | tf_op jit(solution)/shard_map/td,dcm->tcm/dot_general | solution.py:30
  29.2 1.7 all-gather.4.cloned.1.call-done
  30.9 13.2 %copy.14 = bf16[3,640,2240]{2,1,0:T(8,128)(2,1)} copy(bf16[3,640,2240]{1,2,0:T(8,128)(2,1)} %bitcast.84) | data formatting | bytes 17203200 | tf_op jit(solution)/shard_map/td,dcm->tcm/dot_general | solution.py:30
  44.1 8.9 %fusion.10 = bf16[2,256,3,20,32]{1,4,3,2,0:T(8,128)(2,1)S(1)} fusion(bf16[3,20,32,2240,1]{3,2,1,0,4:T(8,128)(2,1)} %bitcast.83, bf16[2,256,2240,1,1]{1,0,2,4,3:T(2,128)(2,1)} %bitcast.88), kind=kOutput, calls=%fused_computation.13 | convolution fusion | flops 4404019200 | bytes 12861440 | tf_op jit(solution)/shard_map/td,dcm->tcm/dot_general | solution.py:30
  53.1 0.3 fusion.18
  53.4 1.9 %fusion.22 = f32[6,20,32,32]{3,0,2,1:T(8,128)S(1)} fusion(f32[2,20,32,32]{3,2,1,0:T(8,128)S(1)} %fusion.18, s32[2]{0:T(128)S(1)} %copy-done.3), kind=kOutput, calls=%fused_computation.30 | convolution fusion | flops 2949132 | bytes 655368 | tf_op jit(solution)/shard_map/si,shef->ihef/dot_general | solution.py:42
  55.4 1.7 copy.20
  57.1 0.0 all-reduce.2.cloned.1.call-update
  57.1 0.0 all-gather.8.cloned.1.call-start
  57.2 0.7 all-gather.8.cloned.1.call-update
  57.8 0.0 all-gather.6.cloned.1.call-start
  57.9 1.3 convert_reduce_fusion.1
  59.2 0.3 fusion.33
  59.6 31.6 %psum.15 = f32[6,20,32]{2,1,0:T(8,128)S(1)} all-reduce(f32[6,20,32]{2,1,0:T(8,128)S(1)} %copy.24), channel_id=1, replica_groups=mesh['groups'=2,'seq'=4,'mp'=2,'rep'=2] {'seq','rep'}, use_global_device_ids=true, to_apply=%region_4.5 | all-reduce | flops 3840 | bytes 30720 | tf_op jit(solution)/shard_map/psum | solution.py:44
  91.2 0.2 convolution_bitcast_fusion.1
  91.4 1.5 fusion.27
  92.9 30.4 %all-reduce.2.cloned.1.call-done = f32[6,20,32,32]{3,2,1,0:T(8,128)} async-done(((f32[6,20,32,32]{3,2,1,0:T(8,128)}), f32[6,20,32,32]{3,2,1,0:T(8,128)}) %all-reduce.2.cloned.1.call-update) | async-done | bytes 491536 | tf_op jit(solution)/shard_map/psum | solution.py:44
  123.3 3.9 %fusion.8 = f32[2,20,32,32]{3,0,2,1:T(2,128)S(1)} fusion(f32[6,20,32,32]{3,2,1,0:T(8,128)} %all-reduce.2.cloned.1.call-done, s32[2]{0:T(128)S(1)} %copy-done.3), kind=kOutput, calls=%fused_computation.11 | convolution fusion | flops 2949132 | bytes 655368 | tf_op jit(solution)/shard_map/si,ihef->shef/dot_general | solution.py:45
  127.2 1.9 %fusion.13 = bf16[2,256,20,32]{1,3,2,0:T(8,128)(2,1)S(1)} fusion(f32[2,20,32,32]{3,0,2,1:T(2,128)S(1)} %fusion.8, f32[2,256,20]{1,2,0:T(8,128)S(1)} %fusion.31, bf16[2,256,3,20,32]{1,4,3,2,0:T(8,128)(2,1)} %copy-done.2), kind=kOutput, calls=%fused_computation.17 | convolution fusion | flops 127467520 | bytes 1515520 | tf_op jit(solution)/shard_map/slhe,shef->slhf/dot_general | solution.py:48
  129.1 0.7 copy.16
  129.8 0.9 copy.36
  130.7 0.0 all-gather.6.cloned.1.call-update
  130.8 0.1 dynamic-slice_bitcast_fusion
  130.8 0.2 copy.11
  131.1 1.3 mul.31
  132.5 1.6 copy.33
  134.1 2.0 %all-gather.8.cloned.1.call-done = bf16[1280,1120]{0,1:T(8,128)(2,1)} async-done(((bf16[640,1120]{0,1:T(8,128)(2,1)}), bf16[1280,1120]{0,1:T(8,128)(2,1)}) %all-gather.8.cloned.1.call-update) | async-done | bytes 2867216 | tf_op jit(solution)/shard_map/all_gather | solution.py:51
  136.1 26.8 %all-gather.6.cloned.1.call-done = bf16[512,1280]{0,1:T(8,128)(2,1)} async-done(((bf16[512,640]{0,1:T(8,128)(2,1)}), bf16[512,1280]{0,1:T(8,128)(2,1)}) %all-gather.6.cloned.1.call-update) | async-done | bytes 1310736 | tf_op jit(solution)/shard_map/all_gather | solution.py:54
  162.9 5.6 %fusion.7 = bf16[512,1120]{0,1:T(8,128)(2,1)} fusion(f32[512,1120]{0,1:T(8,128)} %bitcast.87, bf16[1280,1120]{0,1:T(8,128)(2,1)} %all-gather.8.cloned.1.call-done, bf16[512,1280]{0,1:T(8,128)(2,1)} %all-gather.6.cloned.1.call-done, bf16[512,2240]{0,1:T(8,128)(2,1)S(1)} %copy-done, s32[]{:T(128)S(6)} %select_n.4), kind=kOutput, calls=%fused_computation.10 | convolution fusion | flops 1470300160 | bytes 8765444 | tf_op jit(solution)/shard_map/dot_general | solution.py:53
  (14 shorter events, 0.1 us)
Async XLA Ops:
  6.5 0.9 copy-start.1
  6.5 24.4 %all-gather.4.cloned.1.call-start = ((), (), s32[]{:S(2)}) async-start(), calls=%async_computation | async-start | bytes 12902400 | tf_op jit(solution)/shard_map/all_gather | solution.py:33
  6.5 1.3 copy-start.3
  7.3 116.1 %all-reduce.2.cloned.1.call-start = ((), (), s32[]{:S(2)}) async-start(), calls=%async_computation.1 | async-start | bytes 3932160 | tf_op jit(solution)/shard_map/psum | solution.py:44
  14.2 5.9 %slice-start = ((s8[4587520]{0:T(1024)(128)(4,1)}), s8[4194304]{0:T(1024)(128)(4,1)S(1)}, s32[]{:S(2)}) async-start(s8[4587520]{0:T(1024)(128)(4,1)} %bitcast.76), calls=%async_computation.4 | async-start | bytes 8388608
  17.0 2.1 %copy-start = (bf16[512,2240]{0,1:T(8,128)(2,1)S(1)}, bf16[512,2240]{0,1:T(8,128)(2,1)}, u32[]{:S(2)}) copy-start(bf16[512,2240]{0,1:T(8,128)(2,1)} %param.5) | copy-start | bytes 6881284
  17.0 3.1 %slice-start.1 = ((s8[4587520]{0:T(1024)(128)(4,1)}), s8[393216]{0:T(1024)(128)(4,1)S(1)}, s32[]{:S(2)}) async-start(s8[4587520]{0:T(1024)(128)(4,1)} %bitcast.76), calls=%async_computation.5 | async-start | bytes 786432
  53.1 2.3 %copy-start.2 = (bf16[2,256,3,20,32]{1,4,3,2,0:T(8,128)(2,1)}, bf16[2,256,3,20,32]{1,4,3,2,0:T(8,128)(2,1)S(1)}, u32[]{:S(2)}) copy-start(bf16[2,256,3,20,32]{1,4,3,2,0:T(8,128)(2,1)S(1)} %fusion.10) | copy-start | bytes 5898244
  57.1 79.0 %all-gather.8.cloned.1.call-start = ((), (), s32[]{:S(2)}) async-start(), calls=%async_computation.3 | async-start | bytes 4300800 | tf_op jit(solution)/shard_map/all_gather | solution.py:51
  57.8 105.1 %all-gather.6.cloned.1.call-start = ((), (), s32[]{:S(2)}) async-start(), calls=%async_computation.2 | async-start | bytes 1966080 | tf_op jit(solution)/shard_map/all_gather | solution.py:54
Sparse Core Ops, SparseCore 0:
  8.9 21.9 all-gather.3
  57.2 66.0 all-reduce.1
  124.9 11.1 all-gather.7
  137.5 25.3 all-gather.5
where the time goes:
time: 176 us; the launch traced here: 175 us
  waiting for transfers between devices  62.4 us (35%)
  local copies, waits for them, and re-layouts  37.3 us (21%)
  blocking collectives  31.6 us (18%)
  matrix products  24.9 us (14%)
  between operations  13.3 us (8%)
  other arithmetic  5.39 us (3%)
    psum x1, blocking collectives, body(): state, ksum = lax.psum((state, ksum), ('seq', 'rep'))  31.6 us
    psum x1, waiting for transfers between devices, body(): state, ksum = lax.psum((state, ksum), ('seq', 'rep'))  30.4 us
    all_gather x1, waiting for transfers between devices, body(): lax.all_gather(attn, 'mp', axis=1, tiled=True)  26.8 us
    dot_general x2, local copies, waits for them, and re-layouts, body(): jnp.einsum('td,dcm->tcm', modulated, lax.all_gather(w_qkv, 'rep', axis=0,...  19.3 us
    dot_general x1, matrix products, body(): jnp.einsum('td,dcm->tcm', modulated, lax.all_gather(w_qkv, 'rep', axis=0,...  8.95 us
    unnamed x16, local copies, waits for them, and re-layouts  7.35 us
    dot_general x1, matrix products, body(): jnp.dot(lax.all_gather(attn, 'mp', axis=1, tiled=True), out_full, preferr...  5.59 us
    dot_general x1, matrix products, body(): own_state = jnp.einsum('si,ihef->shef', picker, state, precision=hi)  3.93 us
  transfers between devices with their start and end apart: 4, of which 4 were waited for; matrix products, arithmetic and copies ran while one was open for 19% of the time, Pallas kernels for 0%

commit v1 on v0

--- a/solution.py
+++ b/solution.py
@@ -5,6 +5,18 @@
 
 D = 2240
 HD = 32
+
+
+def collect(x, axis, dim):
+    ways, here = (lax.axis_size(axis), lax.axis_index(axis))
+    grown, reach = (x, 1)
+    while reach < ways:
+        theirs = lax.ppermute(grown, axis, [(d, d ^ reach) for d in range(ways)])
+        mine_first = jnp.concatenate([grown, theirs], axis=dim)
+        theirs_first = jnp.concatenate([theirs, grown], axis=dim)
+        grown = jnp.where(here & reach == 0, mine_first, theirs_first)
+        reach = 2 * reach
+    return grown
 
 
 def body(tokens, slot_image, modulation, w_qkv, w_out):
@@ -50,9 +62,7 @@
     attn = (numer / denom[..., None]).astype(jnp.bfloat16).reshape(rows, per_dev * HD)
     out_full = lax.all_gather(w_out, "rep", axis=0, tiled=True)
     cols = out_full.shape[1]
-    projected = jnp.dot(
-        lax.all_gather(attn, "mp", axis=1, tiled=True), out_full, preferred_element_type=jnp.float32
-    )
+    projected = jnp.dot(collect(attn, "mp", 1), out_full, preferred_element_type=jnp.float32)
     offset = lax.axis_index("mp") * cols
     own_tokens = (
         lax.dynamic_slice_in_dim(tokens, offset, cols, 1)

time: 176 us -> 158 us (0.90)
  waiting for transfers between devices: 62.4 us -> 44.3 us
    all_gather x1 -> x0, waiting for transfers between devices: 26.8 us -> none  [body(): lax.all_gather(attn, 'mp', axis=1, tiled=True)]
    ppermute x0 -> x1, waiting for transfers between devices: none -> 9.19 us  [collect(): theirs = lax.ppermute(grown, axis, [(d, d ^ reach) for d in range(ways)])]
  transfers between devices with their start and end apart: 4 -> 4, of which waited for: 4 -> 4; matrix products, arithmetic and copies ran while one was open for 19% -> 21% of each run, Pallas kernels for 0% -> 0%
where the time goes in v1:
time: 158 us; the launch traced here: 157 us
  waiting for transfers between devices  44.3 us (28%)
  local copies, waits for them, and re-layouts  36.4 us (23%)
  blocking collectives  31.4 us (20%)
  matrix products  24.9 us (16%)
  between operations  13.3 us (8%)
  other arithmetic  5.38 us (3%)
  starting transfers between devices  1.62 us (1%)
    psum x1, blocking collectives, body(): state, ksum = lax.psum((state, ksum), ('seq', 'rep'))  31.4 us
    psum x1, waiting for transfers between devices, body(): state, ksum = lax.psum((state, ksum), ('seq', 'rep'))  30.6 us
    dot_general x2, local copies, waits for them, and re-layouts, body(): jnp.einsum('td,dcm->tcm', modulated, lax.all_gather(w_qkv, 'rep', axis=0,...  19.3 us
    ppermute x1, waiting for transfers between devices, collect(): theirs = lax.ppermute(grown, axis, [(d, d ^ reach) for d in range(ways)])  9.19 us
    dot_general x1, matrix products, body(): jnp.einsum('td,dcm->tcm', modulated, lax.all_gather(w_qkv, 'rep', axis=0,...  8.94 us
    unnamed x16, local copies, waits for them, and re-layouts  6.52 us
    dot_general x1, matrix products, body(): jnp.dot(collect(attn, 'mp', 1), out_full, preferred_element_type=jnp.floa...  5.61 us
    dot_general x1, matrix products, body(): own_state = jnp.einsum('si,ihef->shef', picker, state, precision=hi)  3.93 us
  transfers between devices with their start and end apart: 4, of which 4 were waited for; matrix products, arithmetic and copies ran while one was open for 21% of the time, Pallas kernels for 0%

profile of v1, /device:TPU:0, one launch (start us, length us, event | category | flops | bytes accessed | tf_op | source)
XLA Modules:
  0.0 157.4 jit_solution(15160977016026077519)
XLA Ops:
  6.5 0.7 all-gather.3.cloned.1.call-update
  7.3 0.0 all-reduce.2.cloned.1.call-start
  7.3 0.2 copy-done.1
  7.5 0.2 reshape.54
  7.7 0.1 dot_general.41
  7.8 0.3 fusion.30
  8.1 0.4 copy.12
  8.5 2.7 %mul.34 = f32[2,256,2240]{1,0,2:T(2,128)S(1)} broadcast(f32[2,2240]{0,1:T(8,128)S(1)} %copy.12), dimensions={0,2} | broadcast | bytes 4605440 | tf_op jit(solution)/shard_map/mul | solution.py:38
  11.3 2.6 %copy.34 = f32[280,8,2,256]{3,1,2,0:T(8,128)} copy(f32[280,8,2,256]{3,2,1,0:T(2,128)S(1)} %bitcast.79) | data formatting | bytes 9175040
  13.8 0.4 copy.13
  14.2 0.0 slice-start
  14.2 2.7 %add.57 = f32[2,256,2240]{1,0,2:T(2,128)S(1)} broadcast(f32[2,2240]{0,1:T(8,128)S(1)} %copy.13), dimensions={0,2} | broadcast | bytes 4605440 | tf_op jit(solution)/shard_map/add | solution.py:38
  17.0 0.0 copy-start
  17.0 0.0 slice-start.1
  17.0 0.5 copy.35
  17.5 1.5 copy-done
  19.0 0.4 convert_reduce_fusion
  19.4 0.7 fusion.2
  20.1 0.0 slice-done.1
  20.1 3.0 %fusion.5 = bf16[512,2240]{0,1:T(8,128)(2,1)} fusion(f32[512,2240]{0,1:T(8,128)S(1)} %bitcast.78, f32[512,2240]{0,1:T(8,128)S(1)} %bitcast.77, bf16[512,2240]{0,1:T(8,128)(2,1)S(1)} %copy-done, f32[512]{0:T(512)S(1)} %add_sqrt_fusion, f32[512]{0:T(512)S(1)} %broadcast_multiply_fusion), kind=kLoop, calls=%fused_computation.7 | loop fusion | flops 6881280 | bytes 13766656 | tf_op jit(solution)/shard_map/convert_element_type | solution.py:38
  23.1 6.1 %dot_general.43 = bf16[2,256,2240]{1,0,2:T(2,128)(2,1)} reshape(bf16[512,2240]{0,1:T(8,128)(2,1)} %fusion.5) | data formatting | bytes 4587520 | tf_op jit(solution)/shard_map/td,dcm->tcm/dot_general | solution.py:42
  29.1 1.8 %all-gather.3.cloned.1.call-done = bf16[2240,3,640]{2,0,1:T(8,128)(2,1)} async-done(((bf16[1120,3,640]{2,0,1:T(8,128)(2,1)}), bf16[2240,3,640]{2,0,1:T(8,128)(2,1)}) %all-gather.3.cloned.1.call-update) | async-done | bytes 8601616 | tf_op jit(solution)/shard_map/all_gather | solution.py:45
  30.9 13.2 %copy.14 = bf16[3,640,2240]{2,1,0:T(8,128)(2,1)} copy(bf16[3,640,2240]{1,2,0:T(8,128)(2,1)} %bitcast.83) | data formatting | bytes 17203200 | tf_op jit(solution)/shard_map/td,dcm->tcm/dot_general | solution.py:42
  44.1 8.9 %fusion.10 = bf16[2,256,3,20,32]{1,4,3,2,0:T(8,128)(2,1)S(1)} fusion(bf16[3,20,32,2240,1]{3,2,1,0,4:T(8,128)(2,1)} %bitcast.82, bf16[2,256,2240,1,1]{1,0,2,4,3:T(2,128)(2,1)} %bitcast.86), kind=kOutput, calls=%fused_computation.13 | convolution fusion | flops 4404019200 | bytes 12861440 | tf_op jit(solution)/shard_map/td,dcm->tcm/dot_general | solution.py:42
  53.1 0.3 fusion.24
  53.4 1.9 %fusion.28 = f32[6,20,32,32]{3,0,2,1:T(8,128)S(1)} fusion(f32[2,20,32,32]{3,2,1,0:T(8,128)S(1)} %fusion.24, s32[2]{0:T(128)S(1)} %copy-done.3), kind=kOutput, calls=%fused_computation.37 | convolution fusion | flops 2949132 | bytes 655368 | tf_op jit(solution)/shard_map/si,shef->ihef/dot_general | solution.py:54
  55.4 1.7 %copy.20 = f32[6,20,32,32]{3,2,1,0:T(8,128)} copy(f32[6,20,32,32]{3,0,2,1:T(8,128)S(1)} %fusion.28) | data formatting | bytes 983040 | tf_op jit(solution)/shard_map/si,shef->ihef/dot_general | solution.py:54
  57.1 0.0 all-reduce.2.cloned.1.call-update
  57.1 0.0 all-gather.5.cloned.1.call-start
  57.1 0.7 all-gather.5.cloned.1.call-update
  57.8 1.3 convert_reduce_fusion.1
  59.2 0.3 fusion.39
  59.5 31.4 %psum.15 = f32[6,20,32]{2,1,0:T(8,128)S(1)} all-reduce(f32[6,20,32]{2,1,0:T(8,128)S(1)} %copy.24), channel_id=1, replica_groups=mesh['groups'=2,'seq'=4,'mp'=2,'rep'=2] {'seq','rep'}, use_global_device_ids=true, to_apply=%region_4.5 | all-reduce | flops 3840 | bytes 30720 | tf_op jit(solution)/shard_map/psum | solution.py:56
  90.9 0.2 convolution_bitcast_fusion.1
  91.1 1.5 fusion.33
  92.7 30.6 %all-reduce.2.cloned.1.call-done = f32[6,20,32,32]{3,2,1,0:T(8,128)} async-done(((f32[6,20,32,32]{3,2,1,0:T(8,128)}), f32[6,20,32,32]{3,2,1,0:T(8,128)}) %all-reduce.2.cloned.1.call-update) | async-done | bytes 491536 | tf_op jit(solution)/shard_map/psum | solution.py:56
  123.3 3.9 %fusion.8 = f32[2,20,32,32]{3,0,2,1:T(2,128)S(1)} fusion(f32[6,20,32,32]{3,2,1,0:T(8,128)} %all-reduce.2.cloned.1.call-done, s32[2]{0:T(128)S(1)} %copy-done.3), kind=kOutput, calls=%fused_computation.11 | convolution fusion | flops 2949132 | bytes 655368 | tf_op jit(solution)/shard_map/si,ihef->shef/dot_general | solution.py:57
  127.2 1.9 %fusion.13 = bf16[2,256,20,32]{1,3,2,0:T(8,128)(2,1)S(1)} fusion(f32[2,20,32,32]{3,0,2,1:T(2,128)S(1)} %fusion.8, f32[2,256,20]{1,2,0:T(8,128)S(1)} %fusion.37, bf16[2,256,3,20,32]{1,4,3,2,0:T(8,128)(2,1)} %copy-done.2), kind=kOutput, calls=%fused_computation.17 | convolution fusion | flops 127467520 | bytes 1515520 | tf_op jit(solution)/shard_map/slhe,shef->slhf/dot_general | solution.py:60
  129.1 0.7 copy.16
  129.8 0.1 copy.36
  129.9 1.5 collective-permute-start
  131.4 0.1 dynamic-slice_bitcast_fusion
  131.5 0.2 copy.11
  131.8 1.3 mul.31
  133.1 1.6 %copy.33 = f32[140,8,2,256]{3,1,2,0:T(8,128)} copy(f32[140,8,2,256]{3,2,1,0:T(2,128)S(1)} %bitcast.81) | data formatting | bytes 4587520
  134.7 1.4 all-gather.5.cloned.1.call-done
  136.1 9.2 %collective-permute-done = bf16[512,640]{0,1:T(8,128)(2,1)} collective-permute-done((bf16[512,640]{0,1:T(8,128)(2,1)S(1)}, bf16[512,640]{0,1:T(8,128)(2,1)}, u32[]{:S(2)}, u32[]{:S(2)}) %collective-permute-start) | collective-permute-done | bytes 655392 | tf_op jit(solution)/shard_map/ppermute | solution.py:14
  145.3 5.6 %fusion.7 = bf16[512,1120]{0,1:T(8,128)(2,1)} fusion(f32[512,1120]{0,1:T(8,128)} %bitcast.85, bf16[1280,1120]{0,1:T(8,128)(2,1)} %all-gather.5.cloned.1.call-done, bf16[512,640]{0,1:T(8,128)(2,1)} %collective-permute-done, bf16[512,640]{0,1:T(8,128)(2,1)S(1)} %bitcast.89, pred[]{:T(512)S(6)} %eq.19, bf16[512,2240]{0,1:T(8,128)(2,1)S(1)} %copy-done, ...), kind=kOutput, calls=%fused_computation.10 | convolution fusion | flops 1476198400 | bytes 8765445 | tf_op jit(solution)/shard_map/dot_general | solution.py:65
  (13 shorter events, 0.1 us)
Async XLA Ops:
  6.5 0.9 copy-start.1
  6.5 24.4 %all-gather.3.cloned.1.call-start = ((), (), s32[]{:S(2)}) async-start(), calls=%async_computation | async-start | bytes 12902400 | tf_op jit(solution)/shard_map/all_gather | solution.py:45
  6.5 1.3 copy-start.3
  7.3 116.0 %all-reduce.2.cloned.1.call-start = ((), (), s32[]{:S(2)}) async-start(), calls=%async_computation.1 | async-start | bytes 3932160 | tf_op jit(solution)/shard_map/psum | solution.py:56
  14.2 5.9 %slice-start = ((s8[4587520]{0:T(1024)(128)(4,1)}), s8[4194304]{0:T(1024)(128)(4,1)S(1)}, s32[]{:S(2)}) async-start(s8[4587520]{0:T(1024)(128)(4,1)} %bitcast.75), calls=%async_computation.3 | async-start | bytes 8388608
  17.0 2.1 %copy-start = (bf16[512,2240]{0,1:T(8,128)(2,1)S(1)}, bf16[512,2240]{0,1:T(8,128)(2,1)}, u32[]{:S(2)}) copy-start(bf16[512,2240]{0,1:T(8,128)(2,1)} %param.5) | copy-start | bytes 6881284
  17.0 3.1 %slice-start.1 = ((s8[4587520]{0:T(1024)(128)(4,1)}), s8[393216]{0:T(1024)(128)(4,1)S(1)}, s32[]{:S(2)}) async-start(s8[4587520]{0:T(1024)(128)(4,1)} %bitcast.75), calls=%async_computation.4 | async-start | bytes 786432
  53.1 2.3 %copy-start.2 = (bf16[2,256,3,20,32]{1,4,3,2,0:T(8,128)(2,1)}, bf16[2,256,3,20,32]{1,4,3,2,0:T(8,128)(2,1)S(1)}, u32[]{:S(2)}) copy-start(bf16[2,256,3,20,32]{1,4,3,2,0:T(8,128)(2,1)S(1)} %fusion.10) | copy-start | bytes 5898244
  57.1 79.0 %all-gather.5.cloned.1.call-start = ((), (), s32[]{:S(2)}) async-start(), calls=%async_computation.2 | async-start | bytes 4300800 | tf_op jit(solution)/shard_map/all_gather | solution.py:63
  129.9 15.4 %collective-permute-start = (bf16[512,640]{0,1:T(8,128)(2,1)S(1)}, bf16[512,640]{0,1:T(8,128)(2,1)}, u32[]{:S(2)}, u32[]{:S(2)}) collective-permute-start(bf16[512,640]{0,1:T(8,128)(2,1)S(1)} %bitcast.88), channel_id=1, source_target_pairs={{0,2},{2,0},{1,3},{3,1},{4,6},{6,4},{5,7},{7,5},{8,10},{10,8},{9,1... | collective-permute-start | bytes 1966088 | tf_op jit(solution)/shard_map/ppermute | solution.py:14
Sparse Core Ops, SparseCore 0:
  8.9 21.9 all-gather.2
  57.2 66.0 all-reduce.1
  124.9 11.1 all-gather.4
